TPU v7x, 32 devices: a whole 2x2x4 slice. The times are simulated.
32 devices in a mesh: dp: 8 (over y, x, core), tensor: 4 (over z).
Axes of the slice: x: 2, y: 2, z: 4, core: 2. Of those that a mesh axis runs over, the one named last changes fastest.
Arguments:
- tokens: bfloat16 [5120, 2048], P('dp'), may hold values from -6 to 6
- cotangent: bfloat16 [5120, 2048], P('dp'), may hold values from -6 to 6
- token_slots: int32 [5120], replicated, may hold values from 0 to 8191, as said below
- lengths: int32 [8, 3], P('dp'), may hold values from 0 to 1024, as said below
- mixer_gain: bfloat16 [2048], replicated, may hold values from 0.5 to 1.5
- query_weight: bfloat16 [2048, 1024], P(None, 'tensor'), may hold values from -0.125 to 0.125
- key_weight: bfloat16 [2048, 1024], P(None, 'tensor'), may hold values from -0.125 to 0.125
- value_weight: bfloat16 [2048, 2048], P(None, 'tensor'), may hold values from -0.125 to 0.125
- gate_weight: bfloat16 [2048, 2048], P(None, 'tensor'), may hold values from -0.125 to 0.125
- decay_down: bfloat16 [2048, 16], replicated, may hold values from -0.125 to 0.125
- decay_up: bfloat16 [1024, 16], P('tensor'), may hold values from -1.5 to 1.5
- decay_bias: bfloat16 [1024], P('tensor'), may hold values from -3 to 5
- head_gain: bfloat16 [512], replicated, may hold values from 0.5 to 1.5
- out_weight: bfloat16 [2048, 2048], P('tensor'), may hold values from -0.125 to 0.125
- feed_gain: bfloat16 [2048], replicated, may hold values from 0.5 to 1.5
- feed_gate: bfloat16 [2048, 5632], P(None, 'tensor'), may hold values from -0.125 to 0.125
- feed_up: bfloat16 [2048, 5632], P(None, 'tensor'), may hold values from -0.125 to 0.125
- feed_down: bfloat16 [5632, 2048], P('tensor'), may hold values from -0.078125 to 0.078125
Outputs:
- layer_out: bfloat16 [5120, 2048], P('dp')
- token_grad: bfloat16 [5120, 2048], P('dp')
- grad_mixer_gain: float32 [2048], P('dp')
- grad_query: float32 [2048, 1024], P('dp', 'tensor')
- grad_key: float32 [2048, 1024], P('dp', 'tensor')
- grad_value: float32 [2048, 2048], P('dp', 'tensor')
- grad_gate: float32 [2048, 2048], P('dp', 'tensor')
- grad_decay_down: float32 [2048, 16], P('dp')
- grad_decay_up: float32 [4, 256, 16], P('tensor', 'dp')
- grad_decay_bias: float32 [4, 256], P('tensor', 'dp')
- grad_head_gain: float32 [512], P('dp')
- grad_out: float32 [4, 512, 2048], P('tensor', 'dp')
- grad_feed_gain: float32 [2048], P('dp')
- grad_feed_gate: float32 [2048, 5632], P('dp', 'tensor')
- grad_feed_up: float32 [2048, 5632], P('dp', 'tensor')
- grad_feed_down: float32 [4, 1408, 2048], P('tensor', 'dp')
Inputs may be any that keep to these rules, and one draw needn't show every extreme that they name: `token_slots`: the tokens of one sequence fill consecutive positions of one owner, starting at the sum of the lengths before it; every position below the sum of its owner's lengths receives exactly one token and no position above it; the last owner's positions are all filled; of the 640 tokens of one data device's block at most 128 go to one owner, and some owner receives exactly 128 from every block. The lengths of one owner sum to at most 1024, all lengths together to 5120; a length may be 0; some owner holds one sequence of 1024 tokens.
All inputs are finite; a program needn't handle non-finite values.
Results may differ from a plain program's by a relative error of at most 0.019.
Values may be sent and summed in bfloat16 or wider, within the bound.
A program may use at most 256 MiB of HBM per device.

v0:
```python
import jax
import jax.numpy as jnp
from jax import lax
from jax.sharding import PartitionSpec as P

SPAN = 64
OWN_CAP = 1024
epsilon = 1e-06
head_floor = 1.0
highest_precision = lax.Precision.HIGHEST


def segment_ids(lengths_row, row_count):
    boundary = jnp.cumsum(lengths_row)
    position = jnp.arange(row_count, dtype=jnp.int32)
    return jnp.sum((position[:, None] >= boundary[None, :]).astype(jnp.int32), axis=1)


def norm_rows(row_block, gain_row):
    return (
        row_block
        * lax.rsqrt(jnp.mean(row_block * row_block, axis=-1, keepdims=True) + epsilon)
        * gain_row
    )


def gla_head(query_rows, key_rows, value_rows, gate_logits, out_gate, head_gain, segments):
    row_count = query_rows.shape[0]
    key_width = query_rows.shape[1]
    value_width = value_rows.shape[1]
    blocks = row_count // SPAN
    log_decay = (jax.nn.log_sigmoid(gate_logits) / 16.0).reshape(blocks, SPAN, key_width)
    cumulative = jnp.cumsum(log_decay, axis=1)
    span_total = cumulative[:, SPAN - 1, :]
    queries = (query_rows * float(key_width) ** (-0.5)).reshape(blocks, SPAN, key_width)
    key_block = key_rows.reshape(blocks, SPAN, key_width)
    value_vectors = value_rows.reshape(blocks, SPAN, value_width)
    labels = segments.reshape(blocks, SPAN)
    before = jnp.concatenate([jnp.full((1,), -1, jnp.int32), labels[:-1, SPAN - 1]])
    state_carried_in = (labels == before[:, None]).astype(jnp.float32)
    tail_mask = (labels == labels[:, SPAN - 1 :]).astype(jnp.float32)
    position = jnp.arange(SPAN, dtype=jnp.int32)
    allowed = (position[None, :, None] >= position[None, None, :]) & (
        labels[:, :, None] == labels[:, None, :]
    )
    query_decay_scaled = queries * jnp.exp(cumulative)
    key_grown = key_block * jnp.exp(-cumulative)
    key_final = key_block * jnp.exp(span_total[:, None, :] - cumulative) * tail_mask[:, :, None]
    score_matrix = jnp.einsum(
        "nid,njd->nij", query_decay_scaled, key_grown, precision=highest_precision
    )
    score_matrix = jnp.where(allowed, score_matrix, 0.0)
    inside_span_part = jnp.einsum(
        "kgp,kpc->kgc", score_matrix, value_vectors, precision=highest_precision
    )
    updates = jnp.einsum("njd,nje->nde", key_final, value_vectors, precision=highest_precision)

    def advance(carry_state, inputs):
        update, decay_total, keep_flag = inputs
        return (keep_flag * jnp.exp(decay_total)[:, None] * carry_state + update, carry_state)

    _, state_entering_span = lax.scan(
        advance,
        jnp.zeros((key_width, value_width), jnp.float32),
        (updates, span_total, state_carried_in[:, SPAN - 1]),
    )
    cross_span_part = jnp.einsum(
        "rsm,rmh->rsh",
        query_decay_scaled * state_carried_in[:, :, None],
        state_entering_span,
        precision=highest_precision,
    )
    output = (inside_span_part + cross_span_part).reshape(row_count, value_width)
    scaling = lax.rsqrt(jnp.mean(output * output, axis=-1, keepdims=True) + head_floor)
    return output * scaling * head_gain * jax.nn.silu(out_gate)


def contract_rows(left_mat, right_mat):
    return lax.dot_general(
        left_mat, right_mat, (((0,), (0,)), ((), ())), preferred_element_type=jnp.float32
    )


def times_transposed(left_mat, right_mat):
    return lax.dot_general(
        left_mat, right_mat, (((1,), (1,)), ((), ())), preferred_element_type=jnp.float32
    )


def per_device(
    tokens,
    cotangent,
    token_slots,
    lengths,
    mixer_gain,
    query_weight,
    key_weight,
    value_weight,
    gate_weight,
    decay_down,
    decay_up,
    decay_bias,
    head_gain,
    out_weight,
    feed_gain,
    feed_gate,
    feed_up,
    feed_down,
):
    groups = lax.axis_size("dp")
    member = lax.axis_index("dp")
    local_count = tokens.shape[0]
    model_width = tokens.shape[1]
    peer_cap = OWN_CAP // groups
    my_slots = lax.dynamic_slice_in_dim(token_slots, member * local_count, local_count)
    my_owner = my_slots // OWN_CAP
    owner_ids = jnp.arange(groups, dtype=jnp.int32)
    chosen = (my_owner[:, None] == owner_ids[None, :]).astype(jnp.int32)
    rank_in = jnp.sum((jnp.cumsum(chosen, axis=0) - 1) * chosen, axis=1)
    send_pos = my_owner * peer_cap + rank_in

    def pack_rows(row_block):
        buffer_rows = (
            jnp.zeros((groups * peer_cap, model_width), row_block.dtype).at[send_pos].set(row_block)
        )
        return buffer_rows.reshape(groups, peer_cap, model_width)

    arrived = (
        lax.all_to_all(pack_rows(tokens), "dp", split_axis=0, concat_axis=0, tiled=True),
        lax.all_to_all(pack_rows(cotangent), "dp", split_axis=0, concat_axis=0, tiled=True),
    )
    every_owner = (token_slots // OWN_CAP).reshape(groups, local_count)
    is_mine = (every_owner == member).astype(jnp.int32)
    recv_rank = jnp.cumsum(is_mine, axis=1) - 1
    recv_index = jnp.where(
        is_mine > 0, owner_ids[:, None] * peer_cap + recv_rank, groups * peer_cap
    )
    slot_local = (token_slots % OWN_CAP).reshape(groups, local_count)
    slot_map = (
        jnp.full((groups * peer_cap + 1,), OWN_CAP, jnp.int32)
        .at[recv_index.reshape(-1)]
        .set(slot_local.reshape(-1))[: groups * peer_cap]
    )

    def place_rows(row_block):
        flat_block = row_block.reshape(groups * peer_cap, model_width)
        return (
            jnp.zeros((OWN_CAP + 1, model_width), row_block.dtype)
            .at[slot_map]
            .set(flat_block)[:OWN_CAP]
        )

    def unplace_rows(row_block):
        padded = jnp.concatenate([row_block, jnp.zeros((1, model_width), row_block.dtype)], axis=0)
        return padded[slot_map].reshape(groups, peer_cap, model_width)

    def take_back(returned):
        return returned.reshape(groups * peer_cap, model_width)[send_pos]

    owner_rows = place_rows(arrived[0]).astype(jnp.float32)
    upstream = place_rows(arrived[1])
    labels = segment_ids(lengths[0], OWN_CAP)
    mixed_wide, mixer_norm_back = jax.vjp(norm_rows, owner_rows, mixer_gain.astype(jnp.float32))
    normed = mixed_wide.astype(jnp.bfloat16)

    def project(weight):
        return jnp.dot(normed, weight, preferred_element_type=jnp.float32)

    queries = project(query_weight).astype(jnp.bfloat16)
    keys_low = project(key_weight).astype(jnp.bfloat16)
    value_vectors = project(value_weight).astype(jnp.bfloat16)
    gate_pre = project(gate_weight)
    latent = project(decay_down)
    decay_up_wide = decay_up.astype(jnp.float32)
    logits = lax.dot_general(
        latent, decay_up_wide, (((1,), (1,)), ((), ())), precision=highest_precision
    ) + decay_bias.astype(jnp.float32)

    def mixer(query_wide, key_wide, value_wide, logit_wide, gate_wide, gain_wide):
        return gla_head(query_wide, key_wide, value_wide, logit_wide, gate_wide, gain_wide, labels)

    gated_wide, mixer_back = jax.vjp(
        mixer,
        queries.astype(jnp.float32),
        keys_low.astype(jnp.float32),
        value_vectors.astype(jnp.float32),
        logits,
        gate_pre,
        head_gain.astype(jnp.float32),
    )
    gated_low = gated_wide.astype(jnp.bfloat16)
    mixer_partial = jnp.dot(gated_low, out_weight, preferred_element_type=jnp.float32)
    hidden = owner_rows + lax.psum(mixer_partial, "tensor")
    feed_wide, feed_norm_back = jax.vjp(norm_rows, hidden, feed_gain.astype(jnp.float32))
    feed_normed = feed_wide.astype(jnp.bfloat16)
    gate_hidden = jnp.dot(feed_normed, feed_gate, preferred_element_type=jnp.float32)
    up_hidden = jnp.dot(feed_normed, feed_up, preferred_element_type=jnp.float32)
    sigmoid_gate = jax.nn.sigmoid(gate_hidden)
    swish_gate = gate_hidden * sigmoid_gate
    active = (swish_gate * up_hidden).astype(jnp.bfloat16)
    feed_partial = jnp.dot(active, feed_down, preferred_element_type=jnp.float32)
    layer_rows = (
        hidden + lax.psum(feed_partial.astype(jnp.bfloat16), "tensor").astype(jnp.float32)
    ).astype(jnp.bfloat16)
    upstream_wide = upstream.astype(jnp.float32)
    grad_feed_down = contract_rows(active, upstream)
    d_active = times_transposed(upstream, feed_down)
    d_gate_hidden = (
        d_active * up_hidden * sigmoid_gate * (1.0 + gate_hidden * (1.0 - sigmoid_gate))
    ).astype(jnp.bfloat16)
    d_up_hidden = (d_active * swish_gate).astype(jnp.bfloat16)
    grad_feed_gate = contract_rows(feed_normed, d_gate_hidden)
    grad_feed_up = contract_rows(feed_normed, d_up_hidden)
    feed_part = times_transposed(d_gate_hidden, feed_gate) + times_transposed(d_up_hidden, feed_up)
    d_feed = lax.psum(feed_part, "tensor")
    d_hidden_norm, grad_feed_gain = feed_norm_back(d_feed)
    d_hidden = upstream_wide + d_hidden_norm
    d_mixed = d_hidden.astype(jnp.bfloat16)
    gain_term = jnp.zeros((model_width,), jnp.float32)
    grad_out = contract_rows(gated_low, d_mixed)
    d_gated = times_transposed(d_mixed, out_weight)
    d_query, d_key, d_value, d_logits, d_gate, d_head_gain = mixer_back(d_gated)
    d_query_low = d_query.astype(jnp.bfloat16)
    d_key_low = d_key.astype(jnp.bfloat16)
    d_value_low = d_value.astype(jnp.bfloat16)
    d_gate_low = d_gate.astype(jnp.bfloat16)
    grad_decay_bias = jnp.sum(d_logits, axis=0)
    grad_decay_up = lax.dot_general(
        d_logits, latent, (((0,), (0,)), ((), ())), precision=highest_precision
    )
    latent_part = jnp.dot(d_logits, decay_up_wide, precision=highest_precision)
    mixer_part = (
        times_transposed(d_query_low, query_weight)
        + times_transposed(d_key_low, key_weight)
        + times_transposed(d_value_low, value_weight)
        + times_transposed(d_gate_low, gate_weight)
    )
    summed = lax.psum((mixer_part, latent_part, d_head_gain, gain_term), "tensor")
    d_latent = summed[1]
    d_normed = summed[0] + lax.dot_general(
        d_latent,
        decay_down.astype(jnp.float32),
        (((1,), (1,)), ((), ())),
        precision=highest_precision,
    )
    grad_decay_down = lax.dot_general(
        normed.astype(jnp.float32), d_latent, (((0,), (0,)), ((), ())), precision=highest_precision
    )
    grad_query = contract_rows(normed, d_query_low)
    grad_key = contract_rows(normed, d_key_low)
    grad_value = contract_rows(normed, d_value_low)
    grad_gate = contract_rows(normed, d_gate_low)
    d_rows_norm, grad_mixer_gain = mixer_norm_back(d_normed)
    token_rows = (d_hidden + d_rows_norm).astype(jnp.bfloat16)
    shares = (
        lax.psum_scatter(grad_mixer_gain, "dp", scatter_dimension=0, tiled=True),
        lax.psum_scatter(grad_query, "dp", scatter_dimension=0, tiled=True),
        lax.psum_scatter(grad_key, "dp", scatter_dimension=0, tiled=True),
        lax.psum_scatter(grad_value, "dp", scatter_dimension=0, tiled=True),
        lax.psum_scatter(grad_gate, "dp", scatter_dimension=0, tiled=True),
        lax.psum_scatter(grad_decay_down, "dp", scatter_dimension=0, tiled=True),
        lax.psum_scatter(grad_decay_up, "dp", scatter_dimension=0, tiled=True),
        lax.psum_scatter(grad_decay_bias, "dp", scatter_dimension=0, tiled=True),
        lax.psum_scatter(summed[2], "dp", scatter_dimension=0, tiled=True),
        lax.psum_scatter(grad_out, "dp", scatter_dimension=0, tiled=True),
        lax.psum_scatter(grad_feed_gain, "dp", scatter_dimension=0, tiled=True),
        lax.psum_scatter(grad_feed_gate, "dp", scatter_dimension=0, tiled=True),
        lax.psum_scatter(grad_feed_up, "dp", scatter_dimension=0, tiled=True),
        lax.psum_scatter(grad_feed_down, "dp", scatter_dimension=0, tiled=True),
    )
    returned = (
        lax.all_to_all(unplace_rows(layer_rows), "dp", split_axis=0, concat_axis=0, tiled=True),
        lax.all_to_all(unplace_rows(token_rows), "dp", split_axis=0, concat_axis=0, tiled=True),
    )
    layer_out = take_back(returned[0])
    token_grad = take_back(returned[1])
    rank_width = decay_up.shape[1]
    return (
        layer_out,
        token_grad,
        shares[0],
        shares[1],
        shares[2],
        shares[3],
        shares[4],
        shares[5],
        shares[6].reshape(1, -1, rank_width),
        shares[7].reshape(1, -1),
        shares[8],
        shares[9].reshape(1, shares[9].shape[0], model_width),
        shares[10],
        shares[11],
        shares[12],
        shares[13].reshape(1, shares[13].shape[0], model_width),
    )


def solution(mesh):
    placed = (
        P("dp", None),
        P("dp", None),
        P(),
        P("dp", None),
        P(),
        P(None, "tensor"),
        P(None, "tensor"),
        P(None, "tensor"),
        P(None, "tensor"),
        P(),
        P("tensor", None),
        P("tensor"),
        P(),
        P("tensor", None),
        P(),
        P(None, "tensor"),
        P(None, "tensor"),
        P("tensor", None),
    )
    return jax.shard_map(
        per_device,
        mesh=mesh,
        in_specs=placed,
        out_specs=(
            P("dp", None),
            P("dp", None),
            P("dp"),
            P("dp", "tensor"),
            P("dp", "tensor"),
            P("dp", "tensor"),
            P("dp", "tensor"),
            P("dp", None),
            P("tensor", "dp", None),
            P("tensor", "dp"),
            P("dp"),
            P("tensor", "dp", None),
            P("dp"),
            P("dp", "tensor"),
            P("dp", "tensor"),
            P("tensor", "dp", None),
        ),
        check_vma=False,
    )
```

profile of v0, /device:TPU:0, one launch (start us, length us, event | category | flops | bytes accessed | tf_op | source)
XLA Modules:
  0.0 2135.5 jit_solution(18394428422442927344)
XLA Ops:
  11.7 10.5 scatter_custom_fusion.1
  30.1 19.2 scatter_custom_fusion
  50.7 26.0 %all-to-all-done = bf16[8,128,2048]{2,1,0:T(8,128)(2,1)} async-done(((bf16[8,128,2048]{2,1,0:T(8,128)(2,1)}), bf16[8,128,2048]{2,1,0:T(8,128)(2,1)}, u32[]{:S(2)}, u32[]{:S(2)}) %all-to-all-start) | async-done | bytes 4194336 | tf_op jit(solution)/shard_map/all_to_all | solution.py:129
  120.0 61.8 %while.36 = (s32[]{:T(128)}, f32[256,512]{1,0:T(8,128)S(1)}, f32[16,256,512]{2,1,0:T(8,128)}, f32[16,256]{1,0:T(8,128)S(1)}, f32[16,256,1]{1,2,0:T(1,128)}, /*in...) while((s32[]{:T(128)}, f32[256,512]{1,0:T(8,128)S(1)}, ...), condition=%wide.region_13.14_spmd.clone, body=%wide.region_12.13_spmd.clone.sunk | while | flops 524547 | bytes 2629268 | solution.py:62
  182.4 10.8 multiply_reduce_fusion.4
  206.8 10.9 scatter_custom_fusion.3
  222.5 49.1 %all-to-all-done.2 = bf16[8,128,2048]{2,1,0:T(8,128)(2,1)} async-done(((bf16[8,128,2048]{2,1,0:T(8,128)(2,1)}), bf16[8,128,2048]{2,1,0:T(8,128)(2,1)}, u32[]{:S(2)}, u32[]{:S(2)}) %all-to-all-start.2) | async-done | bytes 4194336 | tf_op jit(solution)/shard_map/all_to_all | solution.py:130
  281.6 216.3 %all-reduce.14.cloned.1.call-done = f32[1024,2048]{1,0:T(8,128)} async-done(((f32[1024,2048]{1,0:T(8,128)}), f32[1024,2048]{1,0:T(8,128)}) %all-reduce.14.cloned.1.call-update) | async-done | bytes 8388624 | tf_op jit(solution)/shard_map/psum | solution.py:193
  506.7 11.9 fusion.87
  518.6 10.3 fusion.86
  528.9 15.1 multiply_convert_fusion.1
  554.2 10.9 convolution_add_fusion.1
  565.2 10.9 convolution_convert_fusion
  576.2 278.9 %all-reduce.18.cloned.1.call-done = f32[1024,2048]{1,0:T(8,128)} async-done(((f32[1024,2048]{1,0:T(8,128)}), f32[1024,2048]{1,0:T(8,128)}) %all-reduce.18.cloned.1.call-update) | async-done | bytes 8388624 | tf_op jit(solution)/shard_map/psum | solution.py:215
  862.7 148.8 %all-reduce.16.cloned.1.call-done = bf16[1024,2048]{1,0:T(8,128)(2,1)} async-done(((bf16[1024,2048]{1,0:T(8,128)(2,1)}), bf16[1024,2048]{1,0:T(8,128)(2,1)}) %all-reduce.16.cloned.1.call-update) | async-done | bytes 4194320 | tf_op jit(solution)/shard_map/psum | solution.py:203
  1011.5 12.5 fusion.6
  1068.5 78.5 %while.37 = (s32[]{:T(128)}, f32[256,512]{1,0:T(8,128)S(1)}, f32[16,256,512]{2,1,0:T(8,128)}, f32[16,256]{1,0:T(8,128)S(1)}, f32[16,256,512]{2,1,0:T(8,128)}, /*...) while((s32[]{:T(128)}, f32[256,512]{1,0:T(8,128)S(1)}, ...), condition=%wide.region_25.26_spmd.clone, body=%wide.region_23.25_spmd.clone.sunk | while | flops 786692 | bytes 3157176 | solution.py:62
  1224.4 254.9 %all-reduce.20.cloned.1.call-done = (f32[1024,2048]{1,0:T(8,128)}, f32[1024,16]{0,1:T(8,128)}) async-done(((f32[1024,2048]{1,0:T(8,128)}, f32[1024,16]{0,1:T(8,128)}), (f32[1024,2048]{1,0:T(8,128)}, f32[1024,16]{0,1:T(8,128)})) %all-reduce.20.cloned.1.call-update) | async-done | bytes 8454160 | tf_op jit(solution)/shard_map/psum | solution.py:238
  1484.0 11.4 fusion.12
  1495.6 11.9 fusion.99
  1507.6 11.9 fusion.98
  1524.3 11.8 gather_fusion
  1558.4 11.6 gather_fusion.2
  1570.0 26.1 %all-to-all-done.1 = bf16[8,128,2048]{2,1,0:T(8,128)(2,1)} async-done(((bf16[8,128,2048]{2,1,0:T(8,128)(2,1)}), bf16[8,128,2048]{2,1,0:T(8,128)(2,1)}, u32[]{:S(2)}, u32[]{:S(2)}) %all-to-all-start.1) | async-done | bytes 4194336 | tf_op jit(solution)/shard_map/all_to_all | solution.py:272
  1614.6 60.6 %all-reduce.7 = (f32[2048]{0:T(1024)S(1)}, f32[256]{0:T(256)S(1)}, f32[512]{0:T(512)S(1)}, f32[2048]{0:T(1024)S(1)}) all-reduce(f32[2048]{0:T(1024)S(1)} %get-tuple-element.304, f32[256]{0:T(256)S(1)} %neg.53, f32[512]{0:T(512)S(1)} %copy-done.70, f32[2048]{0:T(1024)S(1)} %copy-done.62), channel_id=2, replica_groups=mesh['dp'=8,'tensor'=4] {'dp'}, use_global_device_ids=true, to_apply=%region_32.33.clone | all-reduce | flops 4864 | bytes 38912
  1676.5 12.4 psum.48
  1708.0 55.7 %reduce-scatter.19.cloned.1.call-done = f32[256,512]{1,0:T(8,128)} async-done(((f32[2048,512]{1,0:T(8,128)}), f32[256,512]{1,0:T(8,128)}) %reduce-scatter.19.cloned.1.call-update) | async-done | bytes 524304 | tf_op jit(solution)/shard_map/reduce_scatter | solution.py:260
  1763.7 55.1 %reduce-scatter.17.cloned.1.call-done = f32[256,512]{1,0:T(8,128)} async-done(((f32[2048,512]{1,0:T(8,128)}), f32[256,512]{1,0:T(8,128)}) %reduce-scatter.17.cloned.1.call-update) | async-done | bytes 524304 | tf_op jit(solution)/shard_map/reduce_scatter | solution.py:259
  1818.8 37.3 %reduce-scatter.21.cloned.1.call-done = f32[256,16]{0,1:T(8,128)} async-done(((f32[2048,16]{0,1:T(8,128)}), f32[256,16]{0,1:T(8,128)}) %reduce-scatter.21.cloned.1.call-update) | async-done | bytes 16400 | tf_op jit(solution)/shard_map/reduce_scatter | solution.py:261
  1856.0 90.8 %reduce-scatter.29.cloned.1.call-done = f32[176,2048]{1,0:T(8,128)} async-done(((f32[1408,2048]{1,0:T(8,128)}), f32[176,2048]{1,0:T(8,128)}) %reduce-scatter.29.cloned.1.call-update) | async-done | bytes 1441808 | tf_op jit(solution)/shard_map/reduce_scatter | solution.py:269
  1946.8 90.9 %reduce-scatter.27.cloned.1.call-done = f32[256,1408]{1,0:T(8,128)} async-done(((f32[2048,1408]{1,0:T(8,128)}), f32[256,1408]{1,0:T(8,128)}) %reduce-scatter.27.cloned.1.call-update) | async-done | bytes 1441808 | tf_op jit(solution)/shard_map/reduce_scatter | solution.py:268
  2037.7 90.8 %reduce-scatter.25.cloned.1.call-done = f32[256,1408]{1,0:T(8,128)} async-done(((f32[2048,1408]{1,0:T(8,128)}), f32[256,1408]{1,0:T(8,128)}) %reduce-scatter.25.cloned.1.call-update) | async-done | bytes 1441808 | tf_op jit(solution)/shard_map/reduce_scatter | solution.py:267
  (532 shorter events, 441.6 us)
Async XLA Ops:
  7.2 186.1 %copy-start = (bf16[2048,512]{1,0:T(8,128)(2,1)S(1)}, bf16[2048,512]{1,0:T(8,128)(2,1)}, u32[]{:S(2)}) copy-start(bf16[2048,512]{1,0:T(8,128)(2,1)} %param.30) | copy-start | bytes 6291460
  11.7 195.1 %copy-start.64 = (s32[640]{0:T(1024)}, s32[640]{0:T(1024)S(1)}, u32[]{:S(2)}) copy-start(s32[640]{0:T(1024)S(1)} %compare_select_fusion.4) | copy-start | bytes 7684
  22.2 54.5 %all-to-all-start = ((bf16[8,128,2048]{2,1,0:T(8,128)(2,1)}), bf16[8,128,2048]{2,1,0:T(8,128)(2,1)}, u32[]{:S(2)}, u32[]{:S(2)}) async-start(bf16[8,128,2048]{2,1,0:T(8,128)(2,1)} %bitcast.199), calls=%async_computation | async-start | bytes 8388608 | tf_op jit(solution)/shard_map/all_to_all | solution.py:129
  27.5 470.4 %all-reduce.14.cloned.1.call-start = ((), (), s32[]{:S(2)}) async-start(), calls=%async_computation.14 | async-start | bytes 16777216 | tf_op jit(solution)/shard_map/psum | solution.py:193
  28.0 76.0 %copy-start.41 = (s32[16,64]{1,0:T(8,128)}, s32[16,64]{1,0:T(8,128)S(1)}, u32[]{:S(2)}) copy-start(s32[16,64]{1,0:T(8,128)S(1)} %eq.92) | copy-start | bytes 12292
  28.0 62.0 %copy-start.51 = (f32[2048]{0:T(1024)}, f32[2048]{0:T(1024)S(1)}, u32[]{:S(2)}) copy-start(f32[2048]{0:T(1024)S(1)} %convert_element_type.127) | copy-start | bytes 24580
  49.7 54.3 %copy-start.55 = (pred[64,64]{1,0:T(8,128)(4,1)}, pred[64,64]{1,0:T(8,128)(4,1)S(1)}, u32[]{:S(2)}) copy-start(pred[64,64]{1,0:T(8,128)(4,1)S(1)} %iota_compare_fusion) | copy-start | bytes 12292
  49.9 59.0 %copy-start.53 = (f32[16,64]{1,0:T(8,128)}, f32[16,64]{1,0:T(8,128)S(1)}, u32[]{:S(2)}) copy-start(f32[16,64]{1,0:T(8,128)S(1)} %get-tuple-element.369) | copy-start | bytes 12292
  217.7 53.8 %all-to-all-start.2 = ((bf16[8,128,2048]{2,1,0:T(8,128)(2,1)}), bf16[8,128,2048]{2,1,0:T(8,128)(2,1)}, u32[]{:S(2)}, u32[]{:S(2)}) async-start(bf16[8,128,2048]{2,1,0:T(8,128)(2,1)} %bitcast.200), calls=%async_computation.2 | async-start | bytes 8388608 | tf_op jit(solution)/shard_map/all_to_all | solution.py:130
  222.4 632.7 %all-reduce.18.cloned.1.call-start = ((), (), s32[]{:S(2)}) async-start(), calls=%async_computation.16 | async-start | bytes 16777216 | tf_op jit(solution)/shard_map/psum | solution.py:215
  506.7 22.2 %slice-start.6 = ((s8[4227072]{0:T(1024)(128)(4,1)}), s8[4194304]{0:T(1024)(128)(4,1)S(1)}, s32[]{:S(2)}) async-start(s8[4227072]{0:T(1024)(128)(4,1)} %bitcast.191), calls=%async_computation.34 | async-start | bytes 8388608
  565.1 446.4 %all-reduce.16.cloned.1.call-start = ((), (), s32[]{:S(2)}) async-start(), calls=%async_computation.15 | async-start | bytes 8388608 | tf_op jit(solution)/shard_map/psum | solution.py:203
  576.1 903.2 %all-reduce.20.cloned.1.call-start = ((), (), s32[]{:S(2)}) async-start(), calls=%async_computation.27 | async-start | bytes 16908288 | tf_op jit(solution)/shard_map/psum | solution.py:238
  1032.9 25.5 %copy-start.34 = (bf16[1024,512]{1,0:T(8,128)(2,1)}, bf16[1024,512]{1,0:T(8,128)(2,1)S(1)}, u32[]{:S(2)}) copy-start(bf16[1024,512]{1,0:T(8,128)(2,1)S(1)} %get-tuple-element.363) | copy-start | bytes 3145732
  1033.0 16.1 slice-start.2
  1068.5 78.5 %copy-start.14 = (bf16[1024,256]{1,0:T(8,128)(2,1)S(1)}, bf16[1024,256]{1,0:T(8,128)(2,1)}, u32[]{:S(2)}) copy-start(bf16[1024,256]{1,0:T(8,128)(2,1)} %copy-done.12) | copy-start | bytes 1572868
  1068.5 78.5 %copy-start.44 = (f32[16,256]{1,0:T(8,128)S(1)}, f32[16,256]{1,0:T(8,128)}, u32[]{:S(2)}) copy-start(f32[16,256]{1,0:T(8,128)} %copy-done.43) | copy-start | bytes 49156
  1068.5 78.5 %copy-start.54 = (f32[16,64]{1,0:T(8,128)S(1)}, f32[16,64]{1,0:T(8,128)}, u32[]{:S(2)}) copy-start(f32[16,64]{1,0:T(8,128)} %copy-done.53) | copy-start | bytes 12292
  1186.5 417.0 %reduce-scatter.31.cloned.1.call-start = ((), (), s32[]{:S(2)}) async-start(), calls=%async_computation.26 | async-start | bytes 147456
  1189.8 509.6 %reduce-scatter.15.cloned.1.call-start = ((), (), s32[]{:S(2)}) async-start(), calls=%async_computation.18 | async-start | bytes 2359296 | tf_op jit(solution)/shard_map/reduce_scatter | solution.py:258
  1195.6 503.8 %reduce-scatter.13.cloned.1.call-start = ((), (), s32[]{:S(2)}) async-start(), calls=%async_computation.17 | async-start | bytes 2359296 | tf_op jit(solution)/shard_map/reduce_scatter | solution.py:257
  1200.6 507.4 %reduce-scatter.23.cloned.1.call-start = ((), (), s32[]{:S(2)}) async-start(), calls=%async_computation.22 | async-start | bytes 4718592 | tf_op jit(solution)/shard_map/reduce_scatter | solution.py:265
  1208.7 555.0 %reduce-scatter.19.cloned.1.call-start = ((), (), s32[]{:S(2)}) async-start(), calls=%async_computation.20 | async-start | bytes 4718592 | tf_op jit(solution)/shard_map/reduce_scatter | solution.py:260
  1216.6 602.2 %reduce-scatter.17.cloned.1.call-start = ((), (), s32[]{:S(2)}) async-start(), calls=%async_computation.19 | async-start | bytes 4718592 | tf_op jit(solution)/shard_map/reduce_scatter | solution.py:259
  1224.4 631.7 %reduce-scatter.21.cloned.1.call-start = ((), (), s32[]{:S(2)}) async-start(), calls=%async_computation.21 | async-start | bytes 147456 | tf_op jit(solution)/shard_map/reduce_scatter | solution.py:261
  1483.9 462.9 %reduce-scatter.29.cloned.1.call-start = ((), (), s32[]{:S(2)}) async-start(), calls=%async_computation.25 | async-start | bytes 12976128 | tf_op jit(solution)/shard_map/reduce_scatter | solution.py:269
  1495.4 542.3 %reduce-scatter.27.cloned.1.call-start = ((), (), s32[]{:S(2)}) async-start(), calls=%async_computation.24 | async-start | bytes 12976128 | tf_op jit(solution)/shard_map/reduce_scatter | solution.py:268
  1507.6 620.9 %reduce-scatter.25.cloned.1.call-start = ((), (), s32[]{:S(2)}) async-start(), calls=%async_computation.23 | async-start | bytes 12976128 | tf_op jit(solution)/shard_map/reduce_scatter | solution.py:267
  1536.1 13.8 slice-start
  1536.1 60.0 %all-to-all-start.1 = ((bf16[8,128,2048]{2,1,0:T(8,128)(2,1)}), bf16[8,128,2048]{2,1,0:T(8,128)(2,1)}, u32[]{:S(2)}, u32[]{:S(2)}) async-start(bf16[8,128,2048]{2,1,0:T(8,128)(2,1)} %bitcast.198), calls=%async_computation.1 | async-start | bytes 8388608 | tf_op jit(solution)/shard_map/all_to_all | solution.py:272
  1596.1 93.4 %all-to-all-start.3 = ((bf16[8,128,2048]{2,1,0:T(8,128)(2,1)}), bf16[8,128,2048]{2,1,0:T(8,128)(2,1)}, u32[]{:S(2)}, u32[]{:S(2)}) async-start(bf16[8,128,2048]{2,1,0:T(8,128)(2,1)} %bitcast.197), calls=%async_computation.3 | async-start | bytes 8388608 | tf_op jit(solution)/shard_map/all_to_all | solution.py:273
  1689.5 438.9 %copy-start.1 = (bf16[2048,512]{1,0:T(8,128)(2,1)S(1)}, bf16[2048,512]{1,0:T(8,128)(2,1)}, u32[]{:S(2)}) copy-start(bf16[2048,512]{1,0:T(8,128)(2,1)} %param.30) | copy-start | bytes 6291460
  (77 other events, 461.3 us)
Sparse Core Ops, SparseCore 0:
  206.9 290.9 all-reduce.13
  565.2 289.8 all-reduce.17
  857.5 153.9 all-reduce.15
  1186.6 292.6 all-reduce.19
  1482.4 32.3 reduce-scatter.30
  1518.5 60.9 reduce-scatter.14
  1583.7 69.8 reduce-scatter.12
  1657.5 50.4 reduce-scatter.22
  1712.3 51.3 reduce-scatter.18
  1767.4 51.2 reduce-scatter.16
  1822.6 33.3 reduce-scatter.20
  1859.9 86.8 reduce-scatter.28
  1950.9 86.7 reduce-scatter.26
  2041.6 86.7 reduce-scatter.24
where the time goes:
time: 2150 us; the launch traced here: 2140 us
  waiting for transfers between devices  1430 us (67%)
  matrix products  267 us (12%)
  local copies, waits for them, and re-layouts  168 us (8%)
  other arithmetic  159 us (7%)
  blocking collectives  73 us (3%)
    psum x1, waiting for transfers between devices, per_device(): d_feed = lax.psum(feed_part, 'tensor')  279 us
    psum x1, waiting for transfers between devices, per_device(): lax.psum((mixer_part, latent_part, d_head_gain, gain_term), 'tensor')  255 us
    psum x1, waiting for transfers between devices, per_device(): hidden = owner_rows + lax.psum(mixer_partial, 'tensor')  216 us
    psum x1, waiting for transfers between devices, per_device(): lax.psum(feed_partial.astype(jnp.bfloat16), 'tensor').astype(jnp.float32)  149 us
    reduce_scatter x1, waiting for transfers between devices, per_device(): lax.psum_scatter(grad_feed_up, 'dp', scatter_dimension=0, tiled=True)  90.9 us
    reduce_scatter x1, waiting for transfers between devices, per_device(): lax.psum_scatter(grad_feed_down, 'dp', scatter_dimension=0, tiled=True)  90.8 us
    reduce_scatter x1, waiting for transfers between devices, per_device(): lax.psum_scatter(grad_feed_gate, 'dp', scatter_dimension=0, tiled=True)  90.8 us
    dot_general x8, matrix products, contract_rows(): lax.dot_general(left_mat, right_mat, (((0,), (0,)), ((), ())), preferred_...  66.8 us
  transfers between devices with their start and end apart: 18, of which 14 were waited for; matrix products, arithmetic and copies ran while one was open for 10% of the time, Pallas kernels for 0%

commit v1 on v0

--- a/solution.py
+++ b/solution.py
@@ -212,7 +212,9 @@
     grad_feed_gate = contract_rows(feed_normed, d_gate_hidden)
     grad_feed_up = contract_rows(feed_normed, d_up_hidden)
     feed_part = times_transposed(d_gate_hidden, feed_gate) + times_transposed(d_up_hidden, feed_up)
-    d_feed = lax.psum(feed_part, "tensor")
+    d_feed = feed_part
+    for hop in (1, 2):
+        d_feed = d_feed + lax.ppermute(d_feed, "tensor", [(dev, dev ^ hop) for dev in range(4)])
     d_hidden_norm, grad_feed_gain = feed_norm_back(d_feed)
     d_hidden = upstream_wide + d_hidden_norm
     d_mixed = d_hidden.astype(jnp.bfloat16)

time: 2150 us -> 2440 us (1.13)
  waiting for transfers between devices: 1430 us -> 1640 us
  other arithmetic: 159 us -> 241 us
    ppermute x0 -> x2, waiting for transfers between devices: none -> 668 us  [per_device(): lax.ppermute(d_feed, 'tensor', [(dev, dev ^ hop) for dev in range(4)])]
    psum x1 -> x0, waiting for transfers between devices: 279 us -> none  [per_device(): d_feed = lax.psum(feed_part, 'tensor')]
    psum x1, waiting for transfers between devices: 149 us -> 0.01 us  [per_device(): lax.psum(feed_partial.astype(jnp.bfloat16), 'tensor').astype(jnp.float32)]
    reduce_scatter x1, waiting for transfers between devices: 90.8 us -> 3.78 us  [per_device(): lax.psum_scatter(grad_feed_gate, 'dp', scatter_dimension=0, tiled=True)]
    psum x1, waiting for transfers between devices: 255 us -> 197 us  [per_device(): lax.psum((mixer_part, latent_part, d_head_gain, gain_term), 'tensor')]
    reduce_scatter x1, waiting for transfers between devices: 8.56 us -> 55.7 us  [per_device(): lax.psum_scatter(grad_out, 'dp', scatter_dimension=0, tiled=True)]
    reduce_scatter x1, waiting for transfers between devices: 0.01 us -> 45.5 us  [per_device(): lax.psum_scatter(grad_key, 'dp', scatter_dimension=0, tiled=True)]
    reduce_scatter x1, waiting for transfers between devices: 0.01 us -> 45.1 us  [per_device(): lax.psum_scatter(grad_query, 'dp', scatter_dimension=0, tiled=True)]
  transfers between devices with their start and end apart: 18 -> 19, of which waited for: 14 -> 15; matrix products, arithmetic and copies ran while one was open for 10% -> 9% of each run, Pallas kernels for 0% -> 0%
where the time goes in v1:
time: 2440 us; the launch traced here: 2420 us
  waiting for transfers between devices  1640 us (67%)
  matrix products  263 us (11%)
  other arithmetic  241 us (10%)
  local copies, waits for them, and re-layouts  171 us (7%)
  blocking collectives  70 us (3%)
    ppermute x2, waiting for transfers between devices, per_device(): lax.ppermute(d_feed, 'tensor', [(dev, dev ^ hop) for dev in range(4)])  668 us
    psum x1, waiting for transfers between devices, per_device(): hidden = owner_rows + lax.psum(mixer_partial, 'tensor')  217 us
    psum x1, waiting for transfers between devices, per_device(): lax.psum((mixer_part, latent_part, d_head_gain, gain_term), 'tensor')  197 us
    reduce_scatter x1, waiting for transfers between devices, per_device(): lax.psum_scatter(grad_feed_down, 'dp', scatter_dimension=0, tiled=True)  90.9 us
    reduce_scatter x1, waiting for transfers between devices, per_device(): lax.psum_scatter(grad_feed_up, 'dp', scatter_dimension=0, tiled=True)  90.8 us
    dynamic_update_slice x48, other arithmetic, gla_head(): lax.scan(advance, jnp.zeros((key_width, value_width), jnp.float32), (upda...  77.9 us
    dot_general x8, matrix products, contract_rows(): lax.dot_general(left_mat, right_mat, (((0,), (0,)), ((), ())), preferred_...  67.7 us
    dot_general x8, matrix products, times_transposed(): lax.dot_general(left_mat, right_mat, (((1,), (1,)), ((), ())), preferred_...  61.5 us
  transfers between devices with their start and end apart: 19, of which 15 were waited for; matrix products, arithmetic and copies ran while one was open for 9% of the time, Pallas kernels for 0%

profile of v1, /device:TPU:0, one launch (start us, length us, event | category | flops | bytes accessed | tf_op | source)
XLA Modules:
  0.0 2422.0 jit_solution(17156740587101785855)
XLA Ops:
  11.7 10.5 scatter_custom_fusion.1
  30.1 19.2 scatter_custom_fusion
  50.7 26.0 %all-to-all-done = bf16[8,128,2048]{2,1,0:T(8,128)(2,1)} async-done(((bf16[8,128,2048]{2,1,0:T(8,128)(2,1)}), bf16[8,128,2048]{2,1,0:T(8,128)(2,1)}, u32[]{:S(2)}, u32[]{:S(2)}) %all-to-all-start) | async-done | bytes 4194336 | tf_op jit(solution)/shard_map/all_to_all | solution.py:129
  76.7 10.4 scatter_custom_fusion.2
  112.4 92.5 %while.36 = (s32[]{:T(128)}, f32[256,512]{1,0:T(8,128)}, f32[16,256,512]{2,1,0:T(8,128)}, f32[16,256]{1,0:T(8,128)S(1)}, f32[16,256,1]{1,2,0:T(1,128)}, /*index=...) while((s32[]{:T(128)}, f32[256,512]{1,0:T(8,128)}, ...), condition=%wide.region_13.14_spmd.clone, body=%wide.region_12.13_spmd.clone.sunk | while | flops 524547 | bytes 2630276 | solution.py:62
  234.1 10.5 scatter_custom_fusion.3
  249.3 49.1 %all-to-all-done.2 = bf16[8,128,2048]{2,1,0:T(8,128)(2,1)} async-done(((bf16[8,128,2048]{2,1,0:T(8,128)(2,1)}), bf16[8,128,2048]{2,1,0:T(8,128)(2,1)}, u32[]{:S(2)}, u32[]{:S(2)}) %all-to-all-start.2) | async-done | bytes 4194336 | tf_op jit(solution)/shard_map/all_to_all | solution.py:130
  308.5 216.7 %all-reduce.13.cloned.1.call-done = f32[1024,2048]{1,0:T(8,128)} async-done(((f32[1024,2048]{1,0:T(8,128)}), f32[1024,2048]{1,0:T(8,128)}) %all-reduce.13.cloned.1.call-update) | async-done | bytes 8388624 | tf_op jit(solution)/shard_map/psum | solution.py:193
  534.0 11.9 fusion.86
  556.2 15.1 multiply_convert_fusion.1
  593.3 182.3 %collective-permute-done = f32[1024,2048]{1,0:T(8,128)} collective-permute-done((f32[1024,2048]{1,0:T(8,128)S(1)}, f32[1024,2048]{1,0:T(8,128)}, u32[]{:S(2)}, u32[]{:S(2)}) %collective-permute-start) | collective-permute-done | bytes 8388640 | tf_op jit(solution)/shard_map/ppermute | solution.py:217
  775.6 11.8 add.235
  788.9 11.0 convolution_convert_fusion
  800.0 485.3 %collective-permute-done.1 = f32[1024,2048]{1,0:T(8,128)} collective-permute-done((f32[1024,2048]{1,0:T(8,128)}, f32[1024,2048]{1,0:T(8,128)}, u32[]{:S(2)}, u32[]{:S(2)}) %collective-permute-start.1) | collective-permute-done | bytes 8388640 | tf_op jit(solution)/shard_map/ppermute | solution.py:217
  1285.2 10.7 multiply_reduce_fusion
  1296.0 18.3 fusion.6
  1354.2 109.1 %while.37 = (s32[]{:T(128)}, f32[256,512]{1,0:T(8,128)}, f32[16,256,512]{2,1,0:T(8,128)}, f32[16,256]{1,0:T(8,128)S(1)}, f32[16,256,512]{2,1,0:T(8,128)}, /*inde...) while((s32[]{:T(128)}, f32[256,512]{1,0:T(8,128)}, ...), condition=%wide.region_24.25_spmd.clone, body=%wide.region_22.24_spmd.clone.sunk | while | flops 786692 | bytes 3157168 | solution.py:62
  1512.6 12.7 fusion.98
  1525.4 11.9 fusion.99
  1537.4 11.7 fusion.12
  1580.9 11.7 gather_fusion
  1604.6 197.4 %all-reduce.17.cloned.1.call-done = (f32[1024,2048]{1,0:T(8,128)}, f32[1024,16]{0,1:T(8,128)}) async-done(((f32[1024,2048]{1,0:T(8,128)}, f32[1024,16]{0,1:T(8,128)}), (f32[1024,2048]{1,0:T(8,128)}, f32[1024,16]{0,1:T(8,128)})) %all-reduce.17.cloned.1.call-update) | async-done | bytes 8454160 | tf_op jit(solution)/shard_map/psum | solution.py:240
  1819.6 11.6 gather_fusion.2
  1854.5 61.2 %all-reduce.7 = (f32[2048]{0:T(1024)S(1)}, f32[256]{0:T(256)S(1)}, f32[512]{0:T(512)S(1)}, f32[2048]{0:T(1024)S(1)}) all-reduce(f32[2048]{0:T(1024)S(1)} %get-tuple-element.304, f32[256]{0:T(256)S(1)} %neg.53, f32[512]{0:T(512)S(1)} %copy-done.73, f32[2048]{0:T(1024)S(1)} %copy-done.65), channel_id=2, replica_groups=mesh['dp'=8,'tensor'=4] {'dp'}, use_global_device_ids=true, to_apply=%region_31.32.clone | all-reduce | flops 4864 | bytes 38912
  1939.9 90.8 %reduce-scatter.27.cloned.1.call-done = f32[256,1408]{1,0:T(8,128)} async-done(((f32[2048,1408]{1,0:T(8,128)}), f32[256,1408]{1,0:T(8,128)}) %reduce-scatter.27.cloned.1.call-update) | async-done | bytes 1441808 | tf_op jit(solution)/shard_map/reduce_scatter | solution.py:270
  2030.7 90.9 %reduce-scatter.29.cloned.1.call-done = f32[176,2048]{1,0:T(8,128)} async-done(((f32[1408,2048]{1,0:T(8,128)}), f32[176,2048]{1,0:T(8,128)}) %reduce-scatter.29.cloned.1.call-update) | async-done | bytes 1441808 | tf_op jit(solution)/shard_map/reduce_scatter | solution.py:271
  2121.6 45.1 %reduce-scatter.13.cloned.1.call-done = f32[256,256]{1,0:T(8,128)} async-done(((f32[2048,256]{1,0:T(8,128)}), f32[256,256]{1,0:T(8,128)}) %reduce-scatter.13.cloned.1.call-update) | async-done | bytes 262160 | tf_op jit(solution)/shard_map/reduce_scatter | solution.py:259
  2166.6 45.5 %reduce-scatter.15.cloned.1.call-done = f32[256,256]{1,0:T(8,128)} async-done(((f32[2048,256]{1,0:T(8,128)}), f32[256,256]{1,0:T(8,128)}) %reduce-scatter.15.cloned.1.call-update) | async-done | bytes 262160 | tf_op jit(solution)/shard_map/reduce_scatter | solution.py:260
  2212.1 55.1 %reduce-scatter.17.cloned.1.call-done = f32[256,512]{1,0:T(8,128)} async-done(((f32[2048,512]{1,0:T(8,128)}), f32[256,512]{1,0:T(8,128)}) %reduce-scatter.17.cloned.1.call-update) | async-done | bytes 524304 | tf_op jit(solution)/shard_map/reduce_scatter | solution.py:261
  2267.3 55.7 %reduce-scatter.23.cloned.1.call-done = f32[64,2048]{1,0:T(8,128)} async-done(((f32[512,2048]{1,0:T(8,128)}), f32[64,2048]{1,0:T(8,128)}) %reduce-scatter.23.cloned.1.call-update) | async-done | bytes 524304 | tf_op jit(solution)/shard_map/reduce_scatter | solution.py:267
  2322.9 55.1 %reduce-scatter.19.cloned.1.call-done = f32[256,512]{1,0:T(8,128)} async-done(((f32[2048,512]{1,0:T(8,128)}), f32[256,512]{1,0:T(8,128)}) %reduce-scatter.19.cloned.1.call-update) | async-done | bytes 524304 | tf_op jit(solution)/shard_map/reduce_scatter | solution.py:262
  2378.0 37.3 %reduce-scatter.21.cloned.1.call-done = f32[256,16]{0,1:T(8,128)} async-done(((f32[2048,16]{0,1:T(8,128)}), f32[256,16]{0,1:T(8,128)}) %reduce-scatter.21.cloned.1.call-update) | async-done | bytes 16400 | tf_op jit(solution)/shard_map/reduce_scatter | solution.py:263
  (547 shorter events, 521.4 us)
Async XLA Ops:
  7.2 212.9 %copy-start = (bf16[2048,512]{1,0:T(8,128)(2,1)S(1)}, bf16[2048,512]{1,0:T(8,128)(2,1)}, u32[]{:S(2)}) copy-start(bf16[2048,512]{1,0:T(8,128)(2,1)} %param.30) | copy-start | bytes 6291460
  11.7 222.4 %copy-start.67 = (s32[640]{0:T(1024)}, s32[640]{0:T(1024)S(1)}, u32[]{:S(2)}) copy-start(s32[640]{0:T(1024)S(1)} %compare_select_fusion.4) | copy-start | bytes 7684
  22.2 54.5 %all-to-all-start = ((bf16[8,128,2048]{2,1,0:T(8,128)(2,1)}), bf16[8,128,2048]{2,1,0:T(8,128)(2,1)}, u32[]{:S(2)}, u32[]{:S(2)}) async-start(bf16[8,128,2048]{2,1,0:T(8,128)(2,1)} %bitcast.198), calls=%async_computation | async-start | bytes 8388608 | tf_op jit(solution)/shard_map/all_to_all | solution.py:129
  27.5 497.7 %all-reduce.13.cloned.1.call-start = ((), (), s32[]{:S(2)}) async-start(), calls=%async_computation.14 | async-start | bytes 16777216 | tf_op jit(solution)/shard_map/psum | solution.py:193
  30.1 180.4 %copy-start.40 = (s32[16,64]{1,0:T(8,128)}, s32[16,64]{1,0:T(8,128)S(1)}, u32[]{:S(2)}) copy-start(s32[16,64]{1,0:T(8,128)S(1)} %eq.92) | copy-start | bytes 12292
  49.7 160.9 %copy-start.56 = (pred[64,64]{1,0:T(8,128)(4,1)}, pred[64,64]{1,0:T(8,128)(4,1)S(1)}, u32[]{:S(2)}) copy-start(pred[64,64]{1,0:T(8,128)(4,1)S(1)} %iota_compare_fusion) | copy-start | bytes 12292
  49.9 163.5 %copy-start.49 = (f32[16,64]{1,0:T(8,128)}, f32[16,64]{1,0:T(8,128)S(1)}, u32[]{:S(2)}) copy-start(f32[16,64]{1,0:T(8,128)S(1)} %get-tuple-element.370) | copy-start | bytes 12292
  97.2 113.4 %copy-start.2 = (f32[16,64,256]{2,0,1:T(8,128)}, f32[16,64,256]{2,0,1:T(8,128)S(1)}, u32[]{:S(2)}) copy-start(f32[16,64,256]{2,0,1:T(8,128)S(1)} %fusion.51) | copy-start | bytes 3145732
  244.6 53.8 %all-to-all-start.2 = ((bf16[8,128,2048]{2,1,0:T(8,128)(2,1)}), bf16[8,128,2048]{2,1,0:T(8,128)(2,1)}, u32[]{:S(2)}, u32[]{:S(2)}) async-start(bf16[8,128,2048]{2,1,0:T(8,128)(2,1)} %bitcast.199), calls=%async_computation.2 | async-start | bytes 8388608 | tf_op jit(solution)/shard_map/all_to_all | solution.py:130
  249.3 1046.7 %all-reduce.15.cloned.1.call-start = ((), (), s32[]{:S(2)}) async-start(), calls=%async_computation.15 | async-start | bytes 8388608 | tf_op jit(solution)/shard_map/psum | solution.py:203
  593.3 195.5 %copy-start.83 = (bf16[1024,1408]{1,0:T(8,128)(2,1)S(1)}, bf16[1024,1408]{1,0:T(8,128)(2,1)}, u32[]{:S(2)}) copy-start(bf16[1024,1408]{1,0:T(8,128)(2,1)} %get-tuple-element.359) | copy-start | bytes 8650756
  593.3 182.3 %collective-permute-start = (f32[1024,2048]{1,0:T(8,128)S(1)}, f32[1024,2048]{1,0:T(8,128)}, u32[]{:S(2)}, u32[]{:S(2)}) collective-permute-start(f32[1024,2048]{1,0:T(8,128)S(1)} %convolution_add_fusion.1), channel_id=1, source_target_pairs={{0,1},{1,0},{2,3},{3,2},{4,5},{5,4},{6,7},{7,6},{8,9},{9,8},{10,11... | collective-permute-start | bytes 25165832 | tf_op jit(solution)/shard_map/ppermute | solution.py:217
  787.4 497.8 %collective-permute-start.1 = (f32[1024,2048]{1,0:T(8,128)}, f32[1024,2048]{1,0:T(8,128)}, u32[]{:S(2)}, u32[]{:S(2)}) collective-permute-start(f32[1024,2048]{1,0:T(8,128)} %add.235), channel_id=1, source_target_pairs={{0,2},{1,3},{2,0},{3,1},{4,6},{5,7},{6,4},{7,5},{8,10},{9,11},{10,... | collective-permute-start | bytes 25165832 | tf_op jit(solution)/shard_map/ppermute | solution.py:217
  799.9 1002.1 %all-reduce.17.cloned.1.call-start = ((), (), s32[]{:S(2)}) async-start(), calls=%async_computation.26 | async-start | bytes 16908288 | tf_op jit(solution)/shard_map/psum | solution.py:240
  1354.2 109.1 %copy-start.43 = (f32[16,256]{1,0:T(8,128)S(1)}, f32[16,256]{1,0:T(8,128)}, u32[]{:S(2)}) copy-start(f32[16,256]{1,0:T(8,128)} %copy-done.42) | copy-start | bytes 49156
  1354.2 109.1 %copy-start.55 = (f32[16,64]{1,0:T(8,128)S(1)}, f32[16,64]{1,0:T(8,128)}, u32[]{:S(2)}) copy-start(f32[16,64]{1,0:T(8,128)} %copy-done.54) | copy-start | bytes 12292
  1508.9 334.4 %reduce-scatter.31.cloned.1.call-start = ((), (), s32[]{:S(2)}) async-start(), calls=%async_computation.25 | async-start | bytes 147456
  1512.6 427.3 %reduce-scatter.25.cloned.1.call-start = ((), (), s32[]{:S(2)}) async-start(), calls=%async_computation.22 | async-start | bytes 12976128 | tf_op jit(solution)/shard_map/reduce_scatter | solution.py:269
  1525.3 505.3 %reduce-scatter.27.cloned.1.call-start = ((), (), s32[]{:S(2)}) async-start(), calls=%async_computation.23 | async-start | bytes 12976128 | tf_op jit(solution)/shard_map/reduce_scatter | solution.py:270
  1537.4 584.2 %reduce-scatter.29.cloned.1.call-start = ((), (), s32[]{:S(2)}) async-start(), calls=%async_computation.24 | async-start | bytes 12976128 | tf_op jit(solution)/shard_map/reduce_scatter | solution.py:271
  1549.1 617.6 %reduce-scatter.13.cloned.1.call-start = ((), (), s32[]{:S(2)}) async-start(), calls=%async_computation.16 | async-start | bytes 2359296 | tf_op jit(solution)/shard_map/reduce_scatter | solution.py:259
  1554.9 657.2 %reduce-scatter.15.cloned.1.call-start = ((), (), s32[]{:S(2)}) async-start(), calls=%async_computation.17 | async-start | bytes 2359296 | tf_op jit(solution)/shard_map/reduce_scatter | solution.py:260
  1559.9 707.4 %reduce-scatter.17.cloned.1.call-start = ((), (), s32[]{:S(2)}) async-start(), calls=%async_computation.18 | async-start | bytes 4718592 | tf_op jit(solution)/shard_map/reduce_scatter | solution.py:261
  1566.9 756.1 %reduce-scatter.23.cloned.1.call-start = ((), (), s32[]{:S(2)}) async-start(), calls=%async_computation.21 | async-start | bytes 4718592 | tf_op jit(solution)/shard_map/reduce_scatter | solution.py:267
  1592.6 238.6 %all-to-all-start.1 = ((bf16[8,128,2048]{2,1,0:T(8,128)(2,1)}), bf16[8,128,2048]{2,1,0:T(8,128)(2,1)}, u32[]{:S(2)}, u32[]{:S(2)}) async-start(bf16[8,128,2048]{2,1,0:T(8,128)(2,1)} %bitcast.197), calls=%async_computation.1 | async-start | bytes 8388608 | tf_op jit(solution)/shard_map/all_to_all | solution.py:274
  1597.7 780.3 %reduce-scatter.19.cloned.1.call-start = ((), (), s32[]{:S(2)}) async-start(), calls=%async_computation.19 | async-start | bytes 4718592 | tf_op jit(solution)/shard_map/reduce_scatter | solution.py:262
  1597.8 213.3 %slice-start = ((s8[4227072]{0:T(1024)(128)(4,1)}), s8[32768]{0:T(1024)(128)(4,1)S(1)}, s32[]{:S(2)}) async-start(s8[4227072]{0:T(1024)(128)(4,1)} %bitcast.171), calls=%async_computation.27 | async-start | bytes 65536
  1604.6 197.5 %copy-start.47 = (bf16[2048,16]{0,1:T(8,128)(2,1)S(1)}, bf16[2048,16]{0,1:T(8,128)(2,1)}, u32[]{:S(2)}) copy-start(bf16[2048,16]{0,1:T(8,128)(2,1)} %param.31) | copy-start | bytes 196612
  1604.6 197.5 %copy-start.53 = (f32[2048]{0:T(1024)S(1)}, f32[2048]{0:T(1024)}, u32[]{:S(2)}) copy-start(f32[2048]{0:T(1024)} %copy-done.52) | copy-start | bytes 24580
  1604.6 197.5 %copy-start.59 = (f32[1024]{0:T(1024)S(1)}, f32[1024]{0:T(1024)}, u32[]{:S(2)}) copy-start(f32[1024]{0:T(1024)} %copy-done.58) | copy-start | bytes 12292
  1831.2 95.2 %all-to-all-start.3 = ((bf16[8,128,2048]{2,1,0:T(8,128)(2,1)}), bf16[8,128,2048]{2,1,0:T(8,128)(2,1)}, u32[]{:S(2)}, u32[]{:S(2)}) async-start(bf16[8,128,2048]{2,1,0:T(8,128)(2,1)} %bitcast.196), calls=%async_computation.3 | async-start | bytes 8388608 | tf_op jit(solution)/shard_map/all_to_all | solution.py:275
  1835.9 579.4 %reduce-scatter.21.cloned.1.call-start = ((), (), s32[]{:S(2)}) async-start(), calls=%async_computation.20 | async-start | bytes 147456 | tf_op jit(solution)/shard_map/reduce_scatter | solution.py:263
  (84 other events, 628.4 us)
Sparse Core Ops, SparseCore 0:
  234.2 290.9 all-reduce.12
  800.0 384.5 all-reduce.14
  1509.0 292.9 all-reduce.16
  1805.2 32.3 reduce-scatter.30
  1841.5 98.3 reduce-scatter.24
  1943.8 86.7 reduce-scatter.26
  2034.7 86.7 reduce-scatter.28
  2125.4 41.1 reduce-scatter.12
  2170.9 41.2 reduce-scatter.14
  2215.9 51.3 reduce-scatter.16
  2271.6 51.3 reduce-scatter.22
  2326.7 51.2 reduce-scatter.18
  2381.9 33.3 reduce-scatter.20
